TPU v7x, 32 devices: a whole 2x2x4 slice. The times are simulated.
32 devices in a mesh: event: 4 (over z), terrain: 8 (over y, x, core).
Axes of the slice: x: 2, y: 2, z: 4, core: 2. Of those that a mesh axis runs over, the one named last changes fastest.
Arguments:
- level_start: float32 [4, 256, 1024], P('event', 'terrain'), may hold values from -18 to 18
- bed_depth: float32 [256, 1024], P('terrain'), may hold values from 0.5 to 2
- wet_bits: int32 [4, 256, 1024], P('event', 'terrain'), may hold values from 0 to 255
- tile_owner: int32 [2048, 1], P('terrain'), may hold values from 0 to 7; in each aligned block of 256 rows (0 to 255, 256 to 511, ...) at most 48 rows name the same one
- vuln_weight: bfloat16 [128, 256], replicated, may hold values from -0.5 to 0.5
- vuln_bias: float32 [256], replicated, may hold values from -2 to 2
- account_index: int32 [3072, 128], P('terrain'), may hold values from 0 to 1023
- bin_index: int32 [3072, 128], P('terrain'), may hold values from 0 to 255
- exposure_value: bfloat16 [3072, 128], P('terrain'), may hold values from 1 to 10
- deductible: float32 [1024], replicated, may hold values from 0 to 0.8
- limit: float32 [1024], replicated, may hold values from 0.5 to 1.5
Outputs:
- level: float32 [4, 256, 1024], P('event', 'terrain')
- net_loss: bfloat16 [4, 1024, 256], P('event')
- portfolio: float32 [1024, 256], P('terrain')
Inputs may be any that keep to these rules, and one draw needn't show every extreme that they name: `tile_owner`: among the 256 tiles of one device no owner is named more than 48 times; in some devices one owner is named exactly 48 times. `wet_bits`: bit s (the value // 2**s, mod 2) is 1 where the cell is wet in substep s. `account_index`: rows of an owner's records that no tile reaches are not read.
All inputs are finite; a program needn't handle non-finite values.
Results may differ from a plain program's by a relative error of at most 0.0004.
The roundings to bfloat16 on the way count: a program that leaves them out, or rounds other values in their place, can miss the bound.
Values may be sent and summed in bfloat16 or wider, within the bound.
A program may use at most 64 MiB of HBM per device.

v0:
```python
import jax
import jax.numpy as jnp
from jax import lax
from jax.sharding import PartitionSpec as P

SUBSTEPS = 8
courant = 0.5
gravity = 1.0


def with_halo(cells, sides, width):
    for axis, dim in sides:
        count = lax.axis_size(axis)
        ends = count - 1
        head = lax.slice_in_dim(cells, 0, width, axis=dim)
        tail = lax.slice_in_dim(cells, cells.shape[dim] - width, cells.shape[dim], axis=dim)
        cells = jnp.concatenate(
            [
                lax.ppermute(tail, axis, [(i, (i + 1) % count) for i in range(ends)]),
                cells,
                lax.ppermute(head, axis, [((i + 1) % count, i) for i in range(ends)]),
            ],
            axis=dim,
        )
    return cells


def pad_columns(field):
    return jnp.pad(field[:, 1:-1, :], ((0, 0), (0, 0), (1, 1)))


def neighbour_mean(field):
    inner = pad_columns(field)
    return 0.25 * (field[:, 2:, :] + field[:, :-2, :] + inner[:, :, 2:] + inner[:, :, :-2])


def friedrichs_step(level, row_speed, col_speed, bed_depth, wet_factor):
    row_flow = bed_depth * row_speed
    col_flow = pad_columns(bed_depth * col_speed)
    level_pad = pad_columns(level)
    new_level = neighbour_mean(level) - 0.5 * courant * (
        row_flow[:, 2:, :] - row_flow[:, :-2, :] + (col_flow[:, :, 2:] - col_flow[:, :, :-2])
    )
    new_row = (
        neighbour_mean(row_speed) - 0.5 * courant * gravity * (level[:, 2:, :] - level[:, :-2, :])
    ) * wet_factor
    new_col = (
        neighbour_mean(col_speed)
        - 0.5 * courant * gravity * (level_pad[:, :, 2:] - level_pad[:, :, :-2])
    ) * wet_factor
    return (new_level, new_row, new_col)


def per_device(
    level_start,
    bed_depth,
    wet_bits,
    tile_owner,
    vuln_weight,
    vuln_bias,
    account_index,
    bin_index,
    exposure_value,
    deductible,
    limit,
):
    groups, rows, width = level_start.shape
    tile_cells, bin_count = vuln_weight.shape
    account_count = deductible.shape[0]
    owners = lax.axis_size("terrain")
    zeros = jnp.zeros_like(level_start)
    fields = jnp.stack([level_start, zeros, zeros, jnp.broadcast_to(bed_depth, level_start.shape)])
    widened = with_halo(fields, (("terrain", 2),), SUBSTEPS)
    wet_wide = with_halo(wet_bits, (("terrain", 1),), SUBSTEPS)
    level, row_speed, col_speed = (widened[0], widened[1], widened[2])
    bed_wide = widened[3][0]
    first_row = lax.axis_index("terrain") * rows - SUBSTEPS
    total_rows = rows * owners
    for step in range(SUBSTEPS):
        remain = SUBSTEPS - step - 1
        out_rows = rows + 2 * remain
        bed_now = bed_wide[step : step + out_rows + 2]
        row_ids = first_row + step + 1 + jnp.arange(out_rows, dtype=jnp.int32)
        inside = ((row_ids >= 0) & (row_ids < total_rows)).astype(jnp.float32)[None, :, None]
        wet_factor = (wet_wide[:, step + 1 : step + 1 + out_rows] // 2**step % 2).astype(
            jnp.float32
        ) * inside
        level, row_speed, col_speed = friedrichs_step(
            level, row_speed, col_speed, bed_now, wet_factor
        )
        level = level * inside
    pieces = level.astype(jnp.bfloat16).reshape(-1, tile_cells)
    slot_count = account_index.shape[0]
    capacity = slot_count // owners
    owner = tile_owner[:, 0]
    onehot = (owner[:, None] == jnp.arange(owners, dtype=jnp.int32)[None, :]).astype(jnp.int32)
    rank = jnp.sum((jnp.cumsum(onehot, axis=0) - onehot) * onehot, axis=1)
    place = owner * capacity + rank
    chosen = (place[:, None] == jnp.arange(slot_count, dtype=jnp.int32)[None, :]).astype(
        jnp.float32
    )
    marks_out = jnp.sum(chosen, axis=0).astype(jnp.bfloat16).reshape(owners, capacity)
    chosen = chosen.astype(jnp.bfloat16)
    pick = (((0,), (0,)), ((), ()))
    local_ratio = jax.nn.sigmoid(
        jnp.dot(pieces, vuln_weight, preferred_element_type=jnp.float32) + vuln_bias
    ).astype(jnp.bfloat16)
    outgoing = (
        lax.dot_general(chosen, local_ratio, pick, preferred_element_type=jnp.float32)
        .astype(jnp.bfloat16)
        .reshape(owners, capacity, bin_count)
    )
    ratio, marks = (
        lax.all_to_all(outgoing, "terrain", split_axis=0, concat_axis=0, tiled=True),
        lax.all_to_all(marks_out, "terrain", split_axis=0, concat_axis=0, tiled=True),
    )
    weighted = ratio.reshape(slot_count, bin_count) * marks.reshape(slot_count)[:, None]
    block = 32
    bin_range = jnp.arange(bin_count, dtype=jnp.int32)
    share_rows = account_count // owners
    lower = lax.axis_index("terrain") * share_rows
    scale = account_count / (rows * width * owners)
    columns = jnp.arange(account_count, dtype=jnp.int32)

    def add_block(total, block_id):
        first = block_id * block
        account_part = lax.dynamic_slice_in_dim(account_index, first, block, 0).reshape(-1)
        value_part = lax.dynamic_slice_in_dim(exposure_value, first, block, 0).reshape(-1)
        threshold_part = lax.dynamic_slice_in_dim(bin_index, first, block, 0)
        ratio_part = lax.dynamic_slice_in_dim(weighted, first, block, 0)
        left = jnp.where(
            account_part[:, None] == columns[None, :],
            value_part[:, None],
            jnp.zeros((), jnp.bfloat16),
        )
        right = jnp.where(
            bin_range[None, None, :] >= threshold_part[:, :, None],
            ratio_part[:, None, :],
            jnp.zeros((), jnp.bfloat16),
        ).reshape(-1, bin_count)
        return (
            total + lax.dot_general(left, right, pick, preferred_element_type=jnp.float32),
            None,
        )

    total, _ = lax.scan(
        add_block,
        jnp.zeros((account_count, bin_count), jnp.float32),
        jnp.arange(slot_count // block, dtype=jnp.int32),
    )
    whole = lax.psum(total, "terrain")
    net_whole = jnp.minimum(jnp.maximum(whole * scale - deductible[:, None], 0.0), limit[:, None])
    net_loss = net_whole.astype(jnp.bfloat16)[None]
    net_share = lax.dynamic_slice_in_dim(net_whole, lower, share_rows, 0)
    portfolio = lax.psum(net_share, "event") / (groups * lax.axis_size("event"))
    return (level, net_loss, portfolio)


def solution(mesh):
    placed = (
        P("event", "terrain", None),
        P("terrain", None),
        P("event", "terrain", None),
        P("terrain", None),
        P(),
        P(),
        P("terrain", None),
        P("terrain", None),
        P("terrain", None),
        P(),
        P(),
    )
    return jax.shard_map(
        per_device,
        mesh=mesh,
        in_specs=placed,
        out_specs=(P("event", "terrain", None), P("event", None, None), P("terrain", None)),
        check_vma=False,
    )
```

profile of v0, /device:TPU:0, one launch (start us, length us, event | category | flops | bytes accessed | tf_op | source)
XLA Modules:
  0.0 240.6 jit_solution(13161614519495146786)
XLA Ops:
  7.2 0.8 pad_maximum_fusion.3
  8.0 1.3 collective-permute-start.1
  9.3 3.0 %collective-permute-start = (f32[4,1,8,1024]{3,2,1,0:T(8,128)S(1)}, f32[4,1,8,1024]{3,2,1,0:T(8,128)S(1)}, u32[]{:S(2)}, u32[]{:S(2)}) collective-permute-start(f32[4,1,8,1024]{3,2,1,0:T(8,128)S(1)} %get-tuple-element.117), channel_id=1, source_target_pairs={{0,1},{1,2},{2,3},{3,4},{4,5},{5,6},{6,7},{8,9},{9,10},{10,11},{11... | collective-permute-start | bytes 393224 | tf_op jit(solution)/shard_map/ppermute | solution.py:19
  12.4 0.8 fusion.195
  13.2 4.5 %collective-permute-start.2 = (s32[1,8,1024]{2,1,0:T(8,128)S(1)}, s32[1,8,1024]{2,1,0:T(8,128)S(1)}, u32[]{:S(2)}, u32[]{:S(2)}) collective-permute-start(s32[1,8,1024]{2,1,0:T(8,128)S(1)} %get-tuple-element.152), channel_id=1, source_target_pairs={{0,1},{1,2},{2,3},{3,4},{4,5},{5,6},{6,7},{8,9},{9,10},{10,11},{11... | collective-permute-start | bytes 98312 | tf_op jit(solution)/shard_map/ppermute | solution.py:19
  17.7 1.3 collective-permute-start.3
  20.5 0.8 fusion.174
  22.7 5.3 %all-to-all-start.1 = ((bf16[8,1,48]{2,1,0:T(2,128)(2,1)}), bf16[8,1,48]{2,1,0:T(2,128)(2,1)S(1)}, u32[]{:S(2)}, u32[]{:S(2)}) async-start(bf16[8,1,48]{2,1,0:T(2,128)(2,1)} %convert_element_type.186), calls=%async_computation.1 | async-start | bytes 8192 | tf_op jit(solution)/shard_map/all_to_all | solution.py:115
  28.2 0.9 constant_dynamic-update-slice_fusion.1
  29.2 1.0 pad_maximum_fusion
  35.3 0.9 fusion.184
  36.2 1.1 convolution_convert_fusion
  37.3 4.2 %all-to-all-start = ((bf16[8,48,256]{2,1,0:T(8,128)(2,1)}), bf16[8,48,256]{2,1,0:T(8,128)(2,1)S(1)}, u32[]{:S(2)}, u32[]{:S(2)}) async-start(bf16[8,48,256]{2,1,0:T(8,128)(2,1)} %bitcast.19), calls=%async_computation | async-start | bytes 393216 | tf_op jit(solution)/shard_map/all_to_all | solution.py:114
  41.7 6.0 %all-to-all-done = bf16[8,48,256]{2,1,0:T(8,128)(2,1)S(1)} async-done(((bf16[8,48,256]{2,1,0:T(8,128)(2,1)}), bf16[8,48,256]{2,1,0:T(8,128)(2,1)S(1)}, u32[]{:S(2)}, u32[]{:S(2)}) %all-to-all-start) | async-done | bytes 196640 | tf_op jit(solution)/shard_map/all_to_all | solution.py:114
  47.9 90.0 %while.11 = (s32[]{:T(128)}, f32[1024,256]{1,0:T(8,128)S(1)}, s32[12]{0:T(128)S(1)}, s32[384,128]{1,0:T(8,128)}, bf16[384,128]{1,0:T(8,128)(2,1)}, /*index=5*/s3...) while((s32[]{:T(128)}, f32[1024,256]{1,0:T(8,128)S(1)}, ...), condition=%wide.region_5.6_spmd.clone, body=%wide.region_4.5_spmd.clone.sunk | while | flops 2158493696 | bytes 6463685 | solution.py:146
  50.8 4.6 %fusion.203 = f32[1024,256]{1,0:T(8,128)S(1)} fusion(bf16[4096,256]{1,0:T(8,128)(2,1)S(1)} %bitcast.77, s32[4096]{0:T(1024)S(1)} %get-tuple-element.201, s32[4096]{0:T(1024)S(1)} %get-tuple-element.202, bf16[4096]{0:T(1024)(128)(2,1)S(1)} %dynamic-slice_bitcast_fusion.6, f32[1024,256]{1,0:T(8,128)S(1)} %get-tuple-element.215, pred[]{:T(512)S(6)} %compare.53), kind=kOutput, calls=%fused_computation.11.clone.1 | convolution fusion | flops 2158493696 | bytes 4235265 | tf_op jit(solution)/shard_map/while/body/eval_jaxpr/dot_general | solution.py:142
  58.3 4.6 %fusion.203 = f32[1024,256]{1,0:T(8,128)S(1)} fusion(bf16[4096,256]{1,0:T(8,128)(2,1)S(1)} %bitcast.77, s32[4096]{0:T(1024)S(1)} %get-tuple-element.201, s32[4096]{0:T(1024)S(1)} %get-tuple-element.202, bf16[4096]{0:T(1024)(128)(2,1)S(1)} %dynamic-slice_bitcast_fusion.6, f32[1024,256]{1,0:T(8,128)S(1)} %get-tuple-element.215, pred[]{:T(512)S(6)} %compare.53), kind=kOutput, calls=%fused_computation.11.clone.1 | convolution fusion | flops 2158493696 | bytes 4235265 | tf_op jit(solution)/shard_map/while/body/eval_jaxpr/dot_general | solution.py:142
  65.8 4.6 %fusion.203 = f32[1024,256]{1,0:T(8,128)S(1)} fusion(bf16[4096,256]{1,0:T(8,128)(2,1)S(1)} %bitcast.77, s32[4096]{0:T(1024)S(1)} %get-tuple-element.201, s32[4096]{0:T(1024)S(1)} %get-tuple-element.202, bf16[4096]{0:T(1024)(128)(2,1)S(1)} %dynamic-slice_bitcast_fusion.6, f32[1024,256]{1,0:T(8,128)S(1)} %get-tuple-element.215, pred[]{:T(512)S(6)} %compare.53), kind=kOutput, calls=%fused_computation.11.clone.1 | convolution fusion | flops 2158493696 | bytes 4235265 | tf_op jit(solution)/shard_map/while/body/eval_jaxpr/dot_general | solution.py:142
  73.3 4.6 %fusion.203 = f32[1024,256]{1,0:T(8,128)S(1)} fusion(bf16[4096,256]{1,0:T(8,128)(2,1)S(1)} %bitcast.77, s32[4096]{0:T(1024)S(1)} %get-tuple-element.201, s32[4096]{0:T(1024)S(1)} %get-tuple-element.202, bf16[4096]{0:T(1024)(128)(2,1)S(1)} %dynamic-slice_bitcast_fusion.6, f32[1024,256]{1,0:T(8,128)S(1)} %get-tuple-element.215, pred[]{:T(512)S(6)} %compare.53), kind=kOutput, calls=%fused_computation.11.clone.1 | convolution fusion | flops 2158493696 | bytes 4235265 | tf_op jit(solution)/shard_map/while/body/eval_jaxpr/dot_general | solution.py:142
  80.8 4.6 %fusion.203 = f32[1024,256]{1,0:T(8,128)S(1)} fusion(bf16[4096,256]{1,0:T(8,128)(2,1)S(1)} %bitcast.77, s32[4096]{0:T(1024)S(1)} %get-tuple-element.201, s32[4096]{0:T(1024)S(1)} %get-tuple-element.202, bf16[4096]{0:T(1024)(128)(2,1)S(1)} %dynamic-slice_bitcast_fusion.6, f32[1024,256]{1,0:T(8,128)S(1)} %get-tuple-element.215, pred[]{:T(512)S(6)} %compare.53), kind=kOutput, calls=%fused_computation.11.clone.1 | convolution fusion | flops 2158493696 | bytes 4235265 | tf_op jit(solution)/shard_map/while/body/eval_jaxpr/dot_general | solution.py:142
  88.3 4.6 %fusion.203 = f32[1024,256]{1,0:T(8,128)S(1)} fusion(bf16[4096,256]{1,0:T(8,128)(2,1)S(1)} %bitcast.77, s32[4096]{0:T(1024)S(1)} %get-tuple-element.201, s32[4096]{0:T(1024)S(1)} %get-tuple-element.202, bf16[4096]{0:T(1024)(128)(2,1)S(1)} %dynamic-slice_bitcast_fusion.6, f32[1024,256]{1,0:T(8,128)S(1)} %get-tuple-element.215, pred[]{:T(512)S(6)} %compare.53), kind=kOutput, calls=%fused_computation.11.clone.1 | convolution fusion | flops 2158493696 | bytes 4235265 | tf_op jit(solution)/shard_map/while/body/eval_jaxpr/dot_general | solution.py:142
  95.8 4.6 %fusion.203 = f32[1024,256]{1,0:T(8,128)S(1)} fusion(bf16[4096,256]{1,0:T(8,128)(2,1)S(1)} %bitcast.77, s32[4096]{0:T(1024)S(1)} %get-tuple-element.201, s32[4096]{0:T(1024)S(1)} %get-tuple-element.202, bf16[4096]{0:T(1024)(128)(2,1)S(1)} %dynamic-slice_bitcast_fusion.6, f32[1024,256]{1,0:T(8,128)S(1)} %get-tuple-element.215, pred[]{:T(512)S(6)} %compare.53), kind=kOutput, calls=%fused_computation.11.clone.1 | convolution fusion | flops 2158493696 | bytes 4235265 | tf_op jit(solution)/shard_map/while/body/eval_jaxpr/dot_general | solution.py:142
  103.3 4.6 %fusion.203 = f32[1024,256]{1,0:T(8,128)S(1)} fusion(bf16[4096,256]{1,0:T(8,128)(2,1)S(1)} %bitcast.77, s32[4096]{0:T(1024)S(1)} %get-tuple-element.201, s32[4096]{0:T(1024)S(1)} %get-tuple-element.202, bf16[4096]{0:T(1024)(128)(2,1)S(1)} %dynamic-slice_bitcast_fusion.6, f32[1024,256]{1,0:T(8,128)S(1)} %get-tuple-element.215, pred[]{:T(512)S(6)} %compare.53), kind=kOutput, calls=%fused_computation.11.clone.1 | convolution fusion | flops 2158493696 | bytes 4235265 | tf_op jit(solution)/shard_map/while/body/eval_jaxpr/dot_general | solution.py:142
  110.8 4.6 %fusion.203 = f32[1024,256]{1,0:T(8,128)S(1)} fusion(bf16[4096,256]{1,0:T(8,128)(2,1)S(1)} %bitcast.77, s32[4096]{0:T(1024)S(1)} %get-tuple-element.201, s32[4096]{0:T(1024)S(1)} %get-tuple-element.202, bf16[4096]{0:T(1024)(128)(2,1)S(1)} %dynamic-slice_bitcast_fusion.6, f32[1024,256]{1,0:T(8,128)S(1)} %get-tuple-element.215, pred[]{:T(512)S(6)} %compare.53), kind=kOutput, calls=%fused_computation.11.clone.1 | convolution fusion | flops 2158493696 | bytes 4235265 | tf_op jit(solution)/shard_map/while/body/eval_jaxpr/dot_general | solution.py:142
  118.3 4.6 %fusion.203 = f32[1024,256]{1,0:T(8,128)S(1)} fusion(bf16[4096,256]{1,0:T(8,128)(2,1)S(1)} %bitcast.77, s32[4096]{0:T(1024)S(1)} %get-tuple-element.201, s32[4096]{0:T(1024)S(1)} %get-tuple-element.202, bf16[4096]{0:T(1024)(128)(2,1)S(1)} %dynamic-slice_bitcast_fusion.6, f32[1024,256]{1,0:T(8,128)S(1)} %get-tuple-element.215, pred[]{:T(512)S(6)} %compare.53), kind=kOutput, calls=%fused_computation.11.clone.1 | convolution fusion | flops 2158493696 | bytes 4235265 | tf_op jit(solution)/shard_map/while/body/eval_jaxpr/dot_general | solution.py:142
  125.8 4.6 %fusion.203 = f32[1024,256]{1,0:T(8,128)S(1)} fusion(bf16[4096,256]{1,0:T(8,128)(2,1)S(1)} %bitcast.77, s32[4096]{0:T(1024)S(1)} %get-tuple-element.201, s32[4096]{0:T(1024)S(1)} %get-tuple-element.202, bf16[4096]{0:T(1024)(128)(2,1)S(1)} %dynamic-slice_bitcast_fusion.6, f32[1024,256]{1,0:T(8,128)S(1)} %get-tuple-element.215, pred[]{:T(512)S(6)} %compare.53), kind=kOutput, calls=%fused_computation.11.clone.1 | convolution fusion | flops 2158493696 | bytes 4235265 | tf_op jit(solution)/shard_map/while/body/eval_jaxpr/dot_general | solution.py:142
  133.3 4.6 %fusion.203 = f32[1024,256]{1,0:T(8,128)S(1)} fusion(bf16[4096,256]{1,0:T(8,128)(2,1)S(1)} %bitcast.77, s32[4096]{0:T(1024)S(1)} %get-tuple-element.201, s32[4096]{0:T(1024)S(1)} %get-tuple-element.202, bf16[4096]{0:T(1024)(128)(2,1)S(1)} %dynamic-slice_bitcast_fusion.6, f32[1024,256]{1,0:T(8,128)S(1)} %get-tuple-element.215, pred[]{:T(512)S(6)} %compare.53), kind=kOutput, calls=%fused_computation.11.clone.1 | convolution fusion | flops 2158493696 | bytes 4235265 | tf_op jit(solution)/shard_map/while/body/eval_jaxpr/dot_general | solution.py:142
  137.9 1.0 copy-done.1
  139.0 56.2 %all-reduce.33.cloned.1.call-done = f32[1024,256]{1,0:T(8,128)} async-done(((f32[1024,256]{1,0:T(8,128)}), f32[1024,256]{1,0:T(8,128)}) %all-reduce.33.cloned.1.call-update) | async-done | bytes 1048592 | tf_op jit(solution)/shard_map/psum | solution.py:151
  195.2 2.4 convert_bitcast_fusion
  198.2 34.0 %all-reduce.35.cloned.1.call-done = f32[128,256]{1,0:T(8,128)} async-done(((f32[128,256]{1,0:T(8,128)}), f32[128,256]{1,0:T(8,128)}) %all-reduce.35.cloned.1.call-update) | async-done | bytes 131088 | tf_op jit(solution)/shard_map/psum | solution.py:155
  232.2 1.6 broadcast_multiply_fusion
  (144 shorter events, 35.1 us)
Async XLA Ops:
  7.2 29.1 %copy-start = (bf16[128,256]{1,0:T(8,128)(2,1)S(1)}, bf16[128,256]{1,0:T(8,128)(2,1)}, u32[]{:S(2)}) copy-start(bf16[128,256]{1,0:T(8,128)(2,1)} %param.17) | copy-start | bytes 196612
  8.0 21.1 %collective-permute-start.1 = (f32[4,1,8,1024]{3,2,1,0:T(8,128)S(1)}, f32[4,1,8,1024]{3,2,1,0:T(8,128)S(1)}, u32[]{:S(2)}, u32[]{:S(2)}) collective-permute-start(f32[4,1,8,1024]{3,2,1,0:T(8,128)S(1)} %get-tuple-element.118), channel_id=1, source_target_pairs={{1,0},{2,1},{3,2},{4,3},{5,4},{6,5},{7,6},{9,8},{10,9},{11,10},{12... | collective-permute-start | bytes 393224 | tf_op jit(solution)/shard_map/ppermute | solution.py:21
  9.3 19.8 %collective-permute-start = (f32[4,1,8,1024]{3,2,1,0:T(8,128)S(1)}, f32[4,1,8,1024]{3,2,1,0:T(8,128)S(1)}, u32[]{:S(2)}, u32[]{:S(2)}) collective-permute-start(f32[4,1,8,1024]{3,2,1,0:T(8,128)S(1)} %get-tuple-element.117), channel_id=1, source_target_pairs={{0,1},{1,2},{2,3},{3,4},{4,5},{5,6},{6,7},{8,9},{9,10},{10,11},{11... | collective-permute-start | bytes 393224 | tf_op jit(solution)/shard_map/ppermute | solution.py:19
  13.2 15.0 %collective-permute-start.2 = (s32[1,8,1024]{2,1,0:T(8,128)S(1)}, s32[1,8,1024]{2,1,0:T(8,128)S(1)}, u32[]{:S(2)}, u32[]{:S(2)}) collective-permute-start(s32[1,8,1024]{2,1,0:T(8,128)S(1)} %get-tuple-element.152), channel_id=1, source_target_pairs={{0,1},{1,2},{2,3},{3,4},{4,5},{5,6},{6,7},{8,9},{9,10},{10,11},{11... | collective-permute-start | bytes 98312 | tf_op jit(solution)/shard_map/ppermute | solution.py:19
  17.7 11.5 %collective-permute-start.3 = (s32[1,8,1024]{2,1,0:T(8,128)S(1)}, s32[1,8,1024]{2,1,0:T(8,128)S(1)}, u32[]{:S(2)}, u32[]{:S(2)}) collective-permute-start(s32[1,8,1024]{2,1,0:T(8,128)S(1)} %get-tuple-element.151), channel_id=1, source_target_pairs={{1,0},{2,1},{3,2},{4,3},{5,4},{6,5},{7,6},{9,8},{10,9},{11,10},{12... | collective-permute-start | bytes 98312 | tf_op jit(solution)/shard_map/ppermute | solution.py:21
  22.7 14.6 %all-to-all-start.1 = ((bf16[8,1,48]{2,1,0:T(2,128)(2,1)}), bf16[8,1,48]{2,1,0:T(2,128)(2,1)S(1)}, u32[]{:S(2)}, u32[]{:S(2)}) async-start(bf16[8,1,48]{2,1,0:T(2,128)(2,1)} %convert_element_type.186), calls=%async_computation.1 | async-start | bytes 8192 | tf_op jit(solution)/shard_map/all_to_all | solution.py:115
  34.7 1.5 copy-start.4
  37.3 10.4 %all-to-all-start = ((bf16[8,48,256]{2,1,0:T(8,128)(2,1)}), bf16[8,48,256]{2,1,0:T(8,128)(2,1)S(1)}, u32[]{:S(2)}, u32[]{:S(2)}) async-start(bf16[8,48,256]{2,1,0:T(8,128)(2,1)} %bitcast.19), calls=%async_computation | async-start | bytes 393216 | tf_op jit(solution)/shard_map/all_to_all | solution.py:114
  41.5 153.6 %all-reduce.33.cloned.1.call-start = ((), (), s32[]{:S(2)}) async-start(), calls=%async_computation.2 | async-start | bytes 2097152 | tf_op jit(solution)/shard_map/psum | solution.py:151
  47.9 147.3 %copy-start.2 = (f32[1024]{0:T(1024)S(1)}, f32[1024]{0:T(1024)}, u32[]{:S(2)}) copy-start(f32[1024]{0:T(1024)} %param.23) | copy-start | bytes 12292
  47.9 147.3 %copy-start.3 = (f32[1024]{0:T(1024)S(1)}, f32[1024]{0:T(1024)}, u32[]{:S(2)}) copy-start(f32[1024]{0:T(1024)} %param.22) | copy-start | bytes 12292
  137.9 1.0 copy-start.1
  139.0 93.3 %all-reduce.35.cloned.1.call-start = ((), (), s32[]{:S(2)}) async-start(), calls=%async_computation.3 | async-start | bytes 262144 | tf_op jit(solution)/shard_map/psum | solution.py:155
Sparse Core Ops, SparseCore 0:
  139.1 56.0 all-reduce.32
  198.3 33.8 all-reduce.34
where the time goes:
time: 244 us; the launch traced here: 241 us
  waiting for transfers between devices  96.3 us (39%)
  matrix products  56.6 us (23%)
  local copies, waits for them, and re-layouts  31.2 us (13%)
  starting transfers between devices  19.7 us (8%)
  between operations  14.6 us (6%)
  other arithmetic  14 us (6%)
  loops' own time  8.35 us (3%)
    psum x1, waiting for transfers between devices, per_device(): whole = lax.psum(total, 'terrain')  56.2 us
    dot_general x12, matrix products, add_block(): lax.dot_general(left, right, pick, preferred_element_type=jnp.float32)  55.5 us
    psum x1, waiting for transfers between devices, per_device(): portfolio = lax.psum(net_share, 'event') / (groups * lax.axis_size('event'))  34 us
    ge x12, local copies, waits for them, and re-layouts, add_block(): bin_range[None, None, :] >= threshold_part[:, :, None]  8.95 us
    broadcast_in_dim x12, local copies, waits for them, and re-layouts, add_block(): jnp.where(account_part[:, None] == columns[None, :], value_part[:, None],...  8.37 us
    another operation x1, loops' own time, per_device(): lax.scan(add_block, jnp.zeros((account_count, bin_count), jnp.float32), j...  8.35 us
    ppermute x2, starting transfers between devices, with_halo(): lax.ppermute(tail, axis, [(i, (i + 1) % count) for i in range(ends)])  7.51 us
    dynamic_slice x12, local copies, waits for them, and re-layouts, per_device(): lax.scan(add_block, jnp.zeros((account_count, bin_count), jnp.float32), j...  7.04 us
  transfers between devices with their start and end apart: 8, of which 3 were waited for; matrix products, arithmetic and copies ran while one was open for 6% of the time, Pallas kernels for 0%

commit v1 on v0

--- a/solution.py
+++ b/solution.py
@@ -6,6 +6,11 @@
 SUBSTEPS = 8
 courant = 0.5
 gravity = 1.0
+
+
+def add_all(array, mesh_axis):
+    parts = lax.all_gather(array, mesh_axis)
+    return jnp.sum(parts, axis=0)
 
 
 def with_halo(cells, sides, width):
@@ -152,7 +157,7 @@
     net_whole = jnp.minimum(jnp.maximum(whole * scale - deductible[:, None], 0.0), limit[:, None])
     net_loss = net_whole.astype(jnp.bfloat16)[None]
     net_share = lax.dynamic_slice_in_dim(net_whole, lower, share_rows, 0)
-    portfolio = lax.psum(net_share, "event") / (groups * lax.axis_size("event"))
+    portfolio = add_all(net_share, "event") / (groups * lax.axis_size("event"))
     return (level, net_loss, portfolio)
 
 

time: 244 us -> 223 us (0.914)
  waiting for transfers between devices: 96.3 us -> 62.1 us
  blocking collectives: 0 us -> 14.9 us
    psum x1 -> x0, waiting for transfers between devices: 34 us -> none  [per_device(): portfolio = lax.psum(net_share, 'event') / (groups * lax.axis_size('event'))]
    all_gather x0 -> x1, blocking collectives: none -> 14.9 us  [add_all(): parts = lax.all_gather(array, mesh_axis)]
  transfers between devices with their start and end apart: 8 -> 7, of which waited for: 3 -> 2; matrix products, arithmetic and copies ran while one was open for 6% -> 6% of each run, Pallas kernels for 0% -> 0%
where the time goes in v1:
time: 223 us; the launch traced here: 220 us
  waiting for transfers between devices  62.1 us (28%)
  matrix products  56.6 us (25%)
  local copies, waits for them, and re-layouts  30.5 us (14%)
  starting transfers between devices  19.8 us (9%)
  blocking collectives  14.9 us (7%)
  between operations  14.6 us (7%)
  other arithmetic  13.1 us (6%)
  loops' own time  8.35 us (4%)
    psum x1, waiting for transfers between devices, per_device(): whole = lax.psum(total, 'terrain')  56.2 us
    dot_general x12, matrix products, add_block(): lax.dot_general(left, right, pick, preferred_element_type=jnp.float32)  55.5 us
    all_gather x1, blocking collectives, add_all(): parts = lax.all_gather(array, mesh_axis)  14.9 us
    ge x12, local copies, waits for them, and re-layouts, add_block(): bin_range[None, None, :] >= threshold_part[:, :, None]  8.95 us
    broadcast_in_dim x12, local copies, waits for them, and re-layouts, add_block(): jnp.where(account_part[:, None] == columns[None, :], value_part[:, None],...  8.37 us
    another operation x1, loops' own time, per_device(): lax.scan(add_block, jnp.zeros((account_count, bin_count), jnp.float32), j...  8.35 us
    ppermute x2, starting transfers between devices, with_halo(): lax.ppermute(tail, axis, [(i, (i + 1) % count) for i in range(ends)])  7.51 us
    dynamic_slice x12, local copies, waits for them, and re-layouts, per_device(): lax.scan(add_block, jnp.zeros((account_count, bin_count), jnp.float32), j...  7.04 us
  transfers between devices with their start and end apart: 7, of which 2 were waited for; matrix products, arithmetic and copies ran while one was open for 6% of the time, Pallas kernels for 0%

profile of v1, /device:TPU:0, one launch (start us, length us, event | category | flops | bytes accessed | tf_op | source)
XLA Modules:
  0.0 219.9 jit_solution(4470734225177594806)
XLA Ops:
  7.2 0.8 pad_maximum_fusion.3
  8.0 1.3 collective-permute-start.1
  9.3 3.0 %collective-permute-start = (f32[4,1,8,1024]{3,2,1,0:T(8,128)S(1)}, f32[4,1,8,1024]{3,2,1,0:T(8,128)S(1)}, u32[]{:S(2)}, u32[]{:S(2)}) collective-permute-start(f32[4,1,8,1024]{3,2,1,0:T(8,128)S(1)} %get-tuple-element.117), channel_id=1, source_target_pairs={{0,1},{1,2},{2,3},{3,4},{4,5},{5,6},{6,7},{8,9},{9,10},{10,11},{11... | collective-permute-start | bytes 393224 | tf_op jit(solution)/shard_map/ppermute | solution.py:24
  12.4 0.8 fusion.195
  13.2 4.5 %collective-permute-start.2 = (s32[1,8,1024]{2,1,0:T(8,128)S(1)}, s32[1,8,1024]{2,1,0:T(8,128)S(1)}, u32[]{:S(2)}, u32[]{:S(2)}) collective-permute-start(s32[1,8,1024]{2,1,0:T(8,128)S(1)} %get-tuple-element.152), channel_id=1, source_target_pairs={{0,1},{1,2},{2,3},{3,4},{4,5},{5,6},{6,7},{8,9},{9,10},{10,11},{11... | collective-permute-start | bytes 98312 | tf_op jit(solution)/shard_map/ppermute | solution.py:24
  17.7 1.3 collective-permute-start.3
  20.5 0.8 fusion.174
  22.7 5.3 %all-to-all-start.1 = ((bf16[8,1,48]{2,1,0:T(2,128)(2,1)}), bf16[8,1,48]{2,1,0:T(2,128)(2,1)S(1)}, u32[]{:S(2)}, u32[]{:S(2)}) async-start(bf16[8,1,48]{2,1,0:T(2,128)(2,1)} %convert_element_type.186), calls=%async_computation.1 | async-start | bytes 8192 | tf_op jit(solution)/shard_map/all_to_all | solution.py:120
  28.2 0.9 constant_dynamic-update-slice_fusion.1
  29.2 1.0 pad_maximum_fusion
  35.3 0.9 fusion.184
  36.2 1.1 convolution_convert_fusion
  37.3 4.2 %all-to-all-start = ((bf16[8,48,256]{2,1,0:T(8,128)(2,1)}), bf16[8,48,256]{2,1,0:T(8,128)(2,1)S(1)}, u32[]{:S(2)}, u32[]{:S(2)}) async-start(bf16[8,48,256]{2,1,0:T(8,128)(2,1)} %bitcast.19), calls=%async_computation | async-start | bytes 393216 | tf_op jit(solution)/shard_map/all_to_all | solution.py:119
  41.9 5.9 %all-to-all-done = bf16[8,48,256]{2,1,0:T(8,128)(2,1)S(1)} async-done(((bf16[8,48,256]{2,1,0:T(8,128)(2,1)}), bf16[8,48,256]{2,1,0:T(8,128)(2,1)S(1)}, u32[]{:S(2)}, u32[]{:S(2)}) %all-to-all-start) | async-done | bytes 196640 | tf_op jit(solution)/shard_map/all_to_all | solution.py:119
  47.9 90.0 %while.11 = (s32[]{:T(128)}, f32[1024,256]{1,0:T(8,128)S(1)}, s32[12]{0:T(128)S(1)}, s32[384,128]{1,0:T(8,128)}, bf16[384,128]{1,0:T(8,128)(2,1)}, /*index=5*/s3...) while((s32[]{:T(128)}, f32[1024,256]{1,0:T(8,128)S(1)}, ...), condition=%wide.region_5.6_spmd.clone, body=%wide.region_4.5_spmd.clone.sunk | while | flops 2158493696 | bytes 6463685 | solution.py:151
  50.8 4.6 %fusion.203 = f32[1024,256]{1,0:T(8,128)S(1)} fusion(bf16[4096,256]{1,0:T(8,128)(2,1)S(1)} %bitcast.78, s32[4096]{0:T(1024)S(1)} %get-tuple-element.201, s32[4096]{0:T(1024)S(1)} %get-tuple-element.202, bf16[4096]{0:T(1024)(128)(2,1)S(1)} %dynamic-slice_bitcast_fusion.6, f32[1024,256]{1,0:T(8,128)S(1)} %get-tuple-element.215, pred[]{:T(512)S(6)} %compare.53), kind=kOutput, calls=%fused_computation.11.clone.1 | convolution fusion | flops 2158493696 | bytes 4235265 | tf_op jit(solution)/shard_map/while/body/eval_jaxpr/dot_general | solution.py:147
  58.3 4.6 %fusion.203 = f32[1024,256]{1,0:T(8,128)S(1)} fusion(bf16[4096,256]{1,0:T(8,128)(2,1)S(1)} %bitcast.78, s32[4096]{0:T(1024)S(1)} %get-tuple-element.201, s32[4096]{0:T(1024)S(1)} %get-tuple-element.202, bf16[4096]{0:T(1024)(128)(2,1)S(1)} %dynamic-slice_bitcast_fusion.6, f32[1024,256]{1,0:T(8,128)S(1)} %get-tuple-element.215, pred[]{:T(512)S(6)} %compare.53), kind=kOutput, calls=%fused_computation.11.clone.1 | convolution fusion | flops 2158493696 | bytes 4235265 | tf_op jit(solution)/shard_map/while/body/eval_jaxpr/dot_general | solution.py:147
  64.3 0.7 dynamic-slice_bitcast_fusion.5
  65.8 4.6 %fusion.203 = f32[1024,256]{1,0:T(8,128)S(1)} fusion(bf16[4096,256]{1,0:T(8,128)(2,1)S(1)} %bitcast.78, s32[4096]{0:T(1024)S(1)} %get-tuple-element.201, s32[4096]{0:T(1024)S(1)} %get-tuple-element.202, bf16[4096]{0:T(1024)(128)(2,1)S(1)} %dynamic-slice_bitcast_fusion.6, f32[1024,256]{1,0:T(8,128)S(1)} %get-tuple-element.215, pred[]{:T(512)S(6)} %compare.53), kind=kOutput, calls=%fused_computation.11.clone.1 | convolution fusion | flops 2158493696 | bytes 4235265 | tf_op jit(solution)/shard_map/while/body/eval_jaxpr/dot_general | solution.py:147
  73.3 4.6 %fusion.203 = f32[1024,256]{1,0:T(8,128)S(1)} fusion(bf16[4096,256]{1,0:T(8,128)(2,1)S(1)} %bitcast.78, s32[4096]{0:T(1024)S(1)} %get-tuple-element.201, s32[4096]{0:T(1024)S(1)} %get-tuple-element.202, bf16[4096]{0:T(1024)(128)(2,1)S(1)} %dynamic-slice_bitcast_fusion.6, f32[1024,256]{1,0:T(8,128)S(1)} %get-tuple-element.215, pred[]{:T(512)S(6)} %compare.53), kind=kOutput, calls=%fused_computation.11.clone.1 | convolution fusion | flops 2158493696 | bytes 4235265 | tf_op jit(solution)/shard_map/while/body/eval_jaxpr/dot_general | solution.py:147
  80.8 4.6 %fusion.203 = f32[1024,256]{1,0:T(8,128)S(1)} fusion(bf16[4096,256]{1,0:T(8,128)(2,1)S(1)} %bitcast.78, s32[4096]{0:T(1024)S(1)} %get-tuple-element.201, s32[4096]{0:T(1024)S(1)} %get-tuple-element.202, bf16[4096]{0:T(1024)(128)(2,1)S(1)} %dynamic-slice_bitcast_fusion.6, f32[1024,256]{1,0:T(8,128)S(1)} %get-tuple-element.215, pred[]{:T(512)S(6)} %compare.53), kind=kOutput, calls=%fused_computation.11.clone.1 | convolution fusion | flops 2158493696 | bytes 4235265 | tf_op jit(solution)/shard_map/while/body/eval_jaxpr/dot_general | solution.py:147
  88.3 4.6 %fusion.203 = f32[1024,256]{1,0:T(8,128)S(1)} fusion(bf16[4096,256]{1,0:T(8,128)(2,1)S(1)} %bitcast.78, s32[4096]{0:T(1024)S(1)} %get-tuple-element.201, s32[4096]{0:T(1024)S(1)} %get-tuple-element.202, bf16[4096]{0:T(1024)(128)(2,1)S(1)} %dynamic-slice_bitcast_fusion.6, f32[1024,256]{1,0:T(8,128)S(1)} %get-tuple-element.215, pred[]{:T(512)S(6)} %compare.53), kind=kOutput, calls=%fused_computation.11.clone.1 | convolution fusion | flops 2158493696 | bytes 4235265 | tf_op jit(solution)/shard_map/while/body/eval_jaxpr/dot_general | solution.py:147
  95.8 4.6 %fusion.203 = f32[1024,256]{1,0:T(8,128)S(1)} fusion(bf16[4096,256]{1,0:T(8,128)(2,1)S(1)} %bitcast.78, s32[4096]{0:T(1024)S(1)} %get-tuple-element.201, s32[4096]{0:T(1024)S(1)} %get-tuple-element.202, bf16[4096]{0:T(1024)(128)(2,1)S(1)} %dynamic-slice_bitcast_fusion.6, f32[1024,256]{1,0:T(8,128)S(1)} %get-tuple-element.215, pred[]{:T(512)S(6)} %compare.53), kind=kOutput, calls=%fused_computation.11.clone.1 | convolution fusion | flops 2158493696 | bytes 4235265 | tf_op jit(solution)/shard_map/while/body/eval_jaxpr/dot_general | solution.py:147
  103.3 4.6 %fusion.203 = f32[1024,256]{1,0:T(8,128)S(1)} fusion(bf16[4096,256]{1,0:T(8,128)(2,1)S(1)} %bitcast.78, s32[4096]{0:T(1024)S(1)} %get-tuple-element.201, s32[4096]{0:T(1024)S(1)} %get-tuple-element.202, bf16[4096]{0:T(1024)(128)(2,1)S(1)} %dynamic-slice_bitcast_fusion.6, f32[1024,256]{1,0:T(8,128)S(1)} %get-tuple-element.215, pred[]{:T(512)S(6)} %compare.53), kind=kOutput, calls=%fused_computation.11.clone.1 | convolution fusion | flops 2158493696 | bytes 4235265 | tf_op jit(solution)/shard_map/while/body/eval_jaxpr/dot_general | solution.py:147
  110.8 4.6 %fusion.203 = f32[1024,256]{1,0:T(8,128)S(1)} fusion(bf16[4096,256]{1,0:T(8,128)(2,1)S(1)} %bitcast.78, s32[4096]{0:T(1024)S(1)} %get-tuple-element.201, s32[4096]{0:T(1024)S(1)} %get-tuple-element.202, bf16[4096]{0:T(1024)(128)(2,1)S(1)} %dynamic-slice_bitcast_fusion.6, f32[1024,256]{1,0:T(8,128)S(1)} %get-tuple-element.215, pred[]{:T(512)S(6)} %compare.53), kind=kOutput, calls=%fused_computation.11.clone.1 | convolution fusion | flops 2158493696 | bytes 4235265 | tf_op jit(solution)/shard_map/while/body/eval_jaxpr/dot_general | solution.py:147
  118.3 4.6 %fusion.203 = f32[1024,256]{1,0:T(8,128)S(1)} fusion(bf16[4096,256]{1,0:T(8,128)(2,1)S(1)} %bitcast.78, s32[4096]{0:T(1024)S(1)} %get-tuple-element.201, s32[4096]{0:T(1024)S(1)} %get-tuple-element.202, bf16[4096]{0:T(1024)(128)(2,1)S(1)} %dynamic-slice_bitcast_fusion.6, f32[1024,256]{1,0:T(8,128)S(1)} %get-tuple-element.215, pred[]{:T(512)S(6)} %compare.53), kind=kOutput, calls=%fused_computation.11.clone.1 | convolution fusion | flops 2158493696 | bytes 4235265 | tf_op jit(solution)/shard_map/while/body/eval_jaxpr/dot_general | solution.py:147
  125.8 4.6 %fusion.203 = f32[1024,256]{1,0:T(8,128)S(1)} fusion(bf16[4096,256]{1,0:T(8,128)(2,1)S(1)} %bitcast.78, s32[4096]{0:T(1024)S(1)} %get-tuple-element.201, s32[4096]{0:T(1024)S(1)} %get-tuple-element.202, bf16[4096]{0:T(1024)(128)(2,1)S(1)} %dynamic-slice_bitcast_fusion.6, f32[1024,256]{1,0:T(8,128)S(1)} %get-tuple-element.215, pred[]{:T(512)S(6)} %compare.53), kind=kOutput, calls=%fused_computation.11.clone.1 | convolution fusion | flops 2158493696 | bytes 4235265 | tf_op jit(solution)/shard_map/while/body/eval_jaxpr/dot_general | solution.py:147
  133.3 4.6 %fusion.203 = f32[1024,256]{1,0:T(8,128)S(1)} fusion(bf16[4096,256]{1,0:T(8,128)(2,1)S(1)} %bitcast.78, s32[4096]{0:T(1024)S(1)} %get-tuple-element.201, s32[4096]{0:T(1024)S(1)} %get-tuple-element.202, bf16[4096]{0:T(1024)(128)(2,1)S(1)} %dynamic-slice_bitcast_fusion.6, f32[1024,256]{1,0:T(8,128)S(1)} %get-tuple-element.215, pred[]{:T(512)S(6)} %compare.53), kind=kOutput, calls=%fused_computation.11.clone.1 | convolution fusion | flops 2158493696 | bytes 4235265 | tf_op jit(solution)/shard_map/while/body/eval_jaxpr/dot_general | solution.py:147
  137.9 1.0 copy-done.1
  138.9 56.2 %all-reduce.32.cloned.1.call-done = f32[1024,256]{1,0:T(8,128)} async-done(((f32[1024,256]{1,0:T(8,128)}), f32[1024,256]{1,0:T(8,128)}) %all-reduce.32.cloned.1.call-update) | async-done | bytes 1048592 | tf_op jit(solution)/shard_map/psum | solution.py:156
  195.2 2.4 %convert_bitcast_fusion = (bf16[1,1024,256]{2,1,0:T(8,128)(2,1)}, f32[1024,256]{1,0:T(8,128)S(1)}) fusion(f32[1024]{0:T(1024)S(1)} %copy-done.2, f32[1024]{0:T(1024)S(1)} %copy-done.3, f32[1024,256]{1,0:T(8,128)} %all-reduce.32.cloned.1.call-done), kind=kLoop, calls=%fused_computation.29 | loop fusion | flops 1310720 | bytes 2629632 | tf_op jit(solution)/shard_map/broadcast_in_dim | solution.py:158
  197.5 14.9 %all-gather = f32[512,256]{1,0:T(8,128)S(1)} all-gather(f32[128,256]{1,0:T(8,128)S(1)} %constant_dynamic-slice_fusion.1), channel_id=2, replica_groups=mesh['event'=4,'terrain'=8] {'event'}, dimensions={0}, use_global_device_ids=true | all-gather | bytes 655360 | tf_op jit(solution)/shard_map/all_gather | solution.py:12
  (143 shorter events, 34.6 us)
Async XLA Ops:
  7.2 29.1 %copy-start = (bf16[128,256]{1,0:T(8,128)(2,1)S(1)}, bf16[128,256]{1,0:T(8,128)(2,1)}, u32[]{:S(2)}) copy-start(bf16[128,256]{1,0:T(8,128)(2,1)} %param.17) | copy-start | bytes 196612
  8.0 21.1 %collective-permute-start.1 = (f32[4,1,8,1024]{3,2,1,0:T(8,128)S(1)}, f32[4,1,8,1024]{3,2,1,0:T(8,128)S(1)}, u32[]{:S(2)}, u32[]{:S(2)}) collective-permute-start(f32[4,1,8,1024]{3,2,1,0:T(8,128)S(1)} %get-tuple-element.118), channel_id=1, source_target_pairs={{1,0},{2,1},{3,2},{4,3},{5,4},{6,5},{7,6},{9,8},{10,9},{11,10},{12... | collective-permute-start | bytes 393224 | tf_op jit(solution)/shard_map/ppermute | solution.py:26
  9.3 19.8 %collective-permute-start = (f32[4,1,8,1024]{3,2,1,0:T(8,128)S(1)}, f32[4,1,8,1024]{3,2,1,0:T(8,128)S(1)}, u32[]{:S(2)}, u32[]{:S(2)}) collective-permute-start(f32[4,1,8,1024]{3,2,1,0:T(8,128)S(1)} %get-tuple-element.117), channel_id=1, source_target_pairs={{0,1},{1,2},{2,3},{3,4},{4,5},{5,6},{6,7},{8,9},{9,10},{10,11},{11... | collective-permute-start | bytes 393224 | tf_op jit(solution)/shard_map/ppermute | solution.py:24
  13.2 15.0 %collective-permute-start.2 = (s32[1,8,1024]{2,1,0:T(8,128)S(1)}, s32[1,8,1024]{2,1,0:T(8,128)S(1)}, u32[]{:S(2)}, u32[]{:S(2)}) collective-permute-start(s32[1,8,1024]{2,1,0:T(8,128)S(1)} %get-tuple-element.152), channel_id=1, source_target_pairs={{0,1},{1,2},{2,3},{3,4},{4,5},{5,6},{6,7},{8,9},{9,10},{10,11},{11... | collective-permute-start | bytes 98312 | tf_op jit(solution)/shard_map/ppermute | solution.py:24
  17.7 11.5 %collective-permute-start.3 = (s32[1,8,1024]{2,1,0:T(8,128)S(1)}, s32[1,8,1024]{2,1,0:T(8,128)S(1)}, u32[]{:S(2)}, u32[]{:S(2)}) collective-permute-start(s32[1,8,1024]{2,1,0:T(8,128)S(1)} %get-tuple-element.151), channel_id=1, source_target_pairs={{1,0},{2,1},{3,2},{4,3},{5,4},{6,5},{7,6},{9,8},{10,9},{11,10},{12... | collective-permute-start | bytes 98312 | tf_op jit(solution)/shard_map/ppermute | solution.py:26
  22.7 14.6 %all-to-all-start.1 = ((bf16[8,1,48]{2,1,0:T(2,128)(2,1)}), bf16[8,1,48]{2,1,0:T(2,128)(2,1)S(1)}, u32[]{:S(2)}, u32[]{:S(2)}) async-start(bf16[8,1,48]{2,1,0:T(2,128)(2,1)} %convert_element_type.186), calls=%async_computation.1 | async-start | bytes 8192 | tf_op jit(solution)/shard_map/all_to_all | solution.py:120
  34.7 1.5 copy-start.4
  37.3 10.4 %all-to-all-start = ((bf16[8,48,256]{2,1,0:T(8,128)(2,1)}), bf16[8,48,256]{2,1,0:T(8,128)(2,1)S(1)}, u32[]{:S(2)}, u32[]{:S(2)}) async-start(bf16[8,48,256]{2,1,0:T(8,128)(2,1)} %bitcast.19), calls=%async_computation | async-start | bytes 393216 | tf_op jit(solution)/shard_map/all_to_all | solution.py:119
  41.5 153.6 %all-reduce.32.cloned.1.call-start = ((), (), s32[]{:S(2)}) async-start(), calls=%async_computation.2 | async-start | bytes 2097152 | tf_op jit(solution)/shard_map/psum | solution.py:156
  47.9 147.3 %copy-start.2 = (f32[1024]{0:T(1024)S(1)}, f32[1024]{0:T(1024)}, u32[]{:S(2)}) copy-start(f32[1024]{0:T(1024)} %param.23) | copy-start | bytes 12292
  47.9 147.3 %copy-start.3 = (f32[1024]{0:T(1024)S(1)}, f32[1024]{0:T(1024)}, u32[]{:S(2)}) copy-start(f32[1024]{0:T(1024)} %param.22) | copy-start | bytes 12292
  137.9 1.0 copy-start.1
Sparse Core Ops, SparseCore 0:
  139.1 56.0 all-reduce.31
